TPU v7x, 256 devices: a whole 4x4x8 slice. The times are simulated.
256 devices in a mesh: az: 32 (over x, z_hi, core), rad: 8 (over z_lo, y).
Axes of the slice: x: 4, y: 4, z: 8 (z_hi: 4, z_lo: 2; z = z_hi * 2 + z_lo), core: 2. Of those that a mesh axis runs over, the one named last changes fastest.
Arguments:
- fields: float32 [5, 8, 512, 4096], P(None, None, 'rad', 'az'), may hold values from -6 to 6
- velocity: float32 [8, 512, 4096], P(None, 'rad', 'az'), may hold values from -0.5 to 0.5
- shifts: int32 [512], P('rad'), may hold values from 0 to 4095, as said below
- block_inverse: float32 [8, 512, 64], P(None, 'rad'), may hold values from -1 to 1, as said below
- coupling: float32 [8, 8], P(None, 'rad'), may hold values from 0.2 to 0.5
Outputs:
- updated: float32 [5, 8, 512, 4096], P(None, None, 'rad', 'az')
Inputs may be any that keep to these rules, and one draw needn't show every extreme that they name: `shifts`: each radius's shift; the values 0 and 4095 both occur in every draw. `block_inverse`: entries of the given block inverses.
All inputs are finite; a program needn't handle non-finite values.
Results may differ from a plain program's by a relative error of at most 0.000075.
Values sent between devices are 32-bit elements; how exact they have to be, the bound alone decides.
A program may use at most 256 MiB of HBM per device.

v0:
```python
import jax
import jax.numpy as jnp
from jax import lax
from jax.sharding import PartitionSpec as P


def shifted(block, axis, distance):
    devices = range(lax.axis_size(axis))
    route = [((i - distance) % len(devices), i) for i in devices]
    return lax.ppermute(block, axis, route)


def extended(shard, sides, width):
    for axis, dim in sides:
        peers, length = (lax.axis_size(axis), shard.shape[dim])
        up = [(i, (i + 1) % peers) for i in range(peers)]
        down = [(j, i) for i, j in up]
        last = lax.slice_in_dim(shard, length - width, length, axis=dim)
        leading = lax.slice_in_dim(shard, 0, width, axis=dim)
        before = lax.ppermute(last, axis, up)
        after = lax.ppermute(leading, axis, down)
        shard = jnp.concatenate([before, shard, after], axis=dim)
    return shard


def interface_solve(first_row, last_row, top_left, top_right, low_left, low_right, link_rates):
    band_count = link_rates.shape[1]
    crossings = band_count - 1
    nothing = jnp.zeros_like(first_row[:, 0])
    flat_zero = jnp.zeros_like(link_rates[:, :1])
    carry_base = nothing
    carry_slope = flat_zero
    records = []
    for crossing in range(crossings):
        if crossing > 0:
            back_link = (link_rates[:, crossing - 1] * low_left[:, crossing])[:, None]
        else:
            back_link = flat_zero
        self_link = (link_rates[:, crossing] * low_right[:, crossing])[:, None]
        fore_link = (link_rates[:, crossing] * top_left[:, crossing + 1])[:, None]
        if crossing + 1 < crossings:
            next_link = (link_rates[:, crossing + 1] * top_right[:, crossing + 1])[:, None]
        else:
            next_link = flat_zero
        steepness = back_link * carry_slope + self_link
        offset = last_row[:, crossing] + back_link * carry_base
        denominator = 1.0 - fore_link * steepness
        upper_base = (first_row[:, crossing + 1] + fore_link * offset) / denominator
        upper_slope = next_link / denominator
        carry_base = offset + steepness * upper_base
        carry_slope = steepness * upper_slope
        records.append((carry_base, carry_slope, upper_base, upper_slope))
    lower_values = [nothing] * crossings
    upper_values = [nothing] * crossings
    follow = nothing
    for crossing in reversed(range(crossings)):
        carry_base, carry_slope, upper_base, upper_slope = records[crossing]
        lower_values[crossing] = carry_base + carry_slope * follow
        upper_values[crossing] = upper_base + upper_slope * follow
        follow = upper_values[crossing]
    before = jnp.stack([nothing] + lower_values, axis=1)
    beyond = jnp.stack(upper_values + [nothing], axis=1)
    return (before, beyond)


def per_device(fields, velocity, shifts, block_inverse, coupling):
    shard_cells = fields.shape[3]
    shard_hops = shifts // shard_cells
    remainder = shifts - shard_hops * shard_cells
    moving = fields
    sections = (lax.axis_size("az") - 1).bit_length()
    for section in range(sections):
        arrived = shifted(moving, "az", 1 << section)
        chosen = (shard_hops >> section) % 2 == 1
        moving = jnp.where(chosen[None, None, :, None], arrived, moving)
    previous = shifted(moving, "az", 1)
    joined = jnp.concatenate([previous, moving], axis=3)
    rotated = jax.vmap(
        lambda one_row, opening: lax.dynamic_slice_in_dim(one_row, opening, shard_cells, axis=-1),
        in_axes=(2, 0),
        out_axes=2,
    )(joined, shard_cells - remainder)
    stacked = jnp.concatenate([rotated, velocity[None]], axis=0)
    padded = extended(stacked, (("az", 3),), 1)
    values = padded[:5]
    speed = padded[5:]
    outflow = (
        jnp.maximum(speed[..., :-1], 0.0) * values[..., :-1]
        + jnp.minimum(speed[..., :-1], 0.0) * values[..., 1:]
    )
    transported = values[..., 1:-1] - (outflow[..., 1:] - outflow[..., :-1])
    energy = transported[4]
    local_part = jnp.einsum("zrl,zlp->zrp", block_inverse, energy, precision=lax.Precision.HIGHEST)
    corners = jnp.stack(
        [
            block_inverse[:, 0, 0],
            block_inverse[:, 0, -1],
            block_inverse[:, -1, 0],
            block_inverse[:, -1, -1],
        ],
        axis=1,
    )[:, None, :]
    first_all, last_all, corner_all, link_all = (
        lax.all_gather(local_part[:, :1, :], "rad", axis=1, tiled=True),
        lax.all_gather(local_part[:, -1:, :], "rad", axis=1, tiled=True),
        lax.all_gather(corners, "rad", axis=1, tiled=True),
        lax.all_gather(coupling, "rad", axis=1, tiled=True),
    )
    before, beyond = interface_solve(
        first_all,
        last_all,
        corner_all[..., 0],
        corner_all[..., 1],
        corner_all[..., 2],
        corner_all[..., 3],
        link_all,
    )
    band_index = lax.axis_index("rad")
    before_own = lax.dynamic_index_in_dim(before, band_index, 1, keepdims=False)
    beyond_own = lax.dynamic_index_in_dim(beyond, band_index, 1, keepdims=False)
    link_prev = jnp.concatenate([jnp.zeros_like(link_all[:, :1]), link_all[:, :-1]], axis=1)
    prev_own = lax.dynamic_index_in_dim(link_prev, band_index, 1, keepdims=False)
    link_own = coupling[:, 0]
    diffused = (
        local_part
        + (prev_own[:, None] * block_inverse[:, :, 0])[:, :, None] * before_own[:, None, :]
        + (link_own[:, None] * block_inverse[:, :, -1])[:, :, None] * beyond_own[:, None, :]
    )
    return jnp.concatenate([transported[:4], diffused[None]], axis=0)


def solution(mesh):
    placed = (
        P(None, None, "rad", "az"),
        P(None, "rad", "az"),
        P("rad"),
        P(None, "rad", None),
        P(None, "rad"),
    )
    return jax.shard_map(
        per_device,
        mesh=mesh,
        in_specs=placed,
        out_specs=P(None, None, "rad", "az"),
        check_vma=False,
    )
```

profile of v0, /device:TPU:0, one launch (start us, length us, event | category | flops | bytes accessed | tf_op | source)
XLA Modules:
  0.0 436.5 jit_solution(17480261281971726092)
XLA Ops:
  0.0 0.7 fusion.23
  0.7 25.5 %collective-permute-done = f32[5,8,64,128]{3,2,1,0:T(8,128)S(1)} collective-permute-done((f32[5,8,64,128]{3,2,1,0:T(8,128)}, f32[5,8,64,128]{3,2,1,0:T(8,128)S(1)}, u32[]{:S(2)}, u32[]{:S(2)}) %collective-permute-start) | collective-permute-done | bytes 1310752 | tf_op jit(solution)/shard_map/ppermute | solution.py:10
  26.2 1.6 broadcast_select_fusion
  27.9 38.1 %collective-permute-done.1 = f32[5,8,64,128]{3,2,1,0:T(8,128)S(1)} collective-permute-done((f32[5,8,64,128]{3,2,1,0:T(8,128)S(1)}, f32[5,8,64,128]{3,2,1,0:T(8,128)S(1)}, u32[]{:S(2)}, u32[]{:S(2)}) %collective-permute-start.1) | collective-permute-done | bytes 1310752 | tf_op jit(solution)/shard_map/ppermute | solution.py:10
  66.3 40.9 %collective-permute-start.2 = (f32[5,8,64,128]{3,2,1,0:T(8,128)S(1)}, f32[5,8,64,128]{3,2,1,0:T(8,128)S(1)}, u32[]{:S(2)}, u32[]{:S(2)}) collective-permute-start(f32[5,8,64,128]{3,2,1,0:T(8,128)S(1)} %broadcast_select_fusion.1), channel_id=1, source_target_pairs={{224,0},{232,8},{240,16},{248,24},{0,32},{8,40},{16,48},{24,56},{3... | collective-permute-start | bytes 3932168 | tf_op jit(solution)/shard_map/ppermute | solution.py:10
  107.1 32.1 %collective-permute-done.2 = f32[5,8,64,128]{3,2,1,0:T(8,128)S(1)} collective-permute-done((f32[5,8,64,128]{3,2,1,0:T(8,128)S(1)}, f32[5,8,64,128]{3,2,1,0:T(8,128)S(1)}, u32[]{:S(2)}, u32[]{:S(2)}) %collective-permute-start.2) | collective-permute-done | bytes 1310752 | tf_op jit(solution)/shard_map/ppermute | solution.py:10
  139.7 40.0 %collective-permute-done.3 = f32[5,8,64,128]{3,2,1,0:T(8,128)S(1)} collective-permute-done((f32[5,8,64,128]{3,2,1,0:T(8,128)S(1)}, f32[5,8,64,128]{3,2,1,0:T(8,128)S(1)}, u32[]{:S(2)}, u32[]{:S(2)}) %collective-permute-start.3) | collective-permute-done | bytes 1310752 | tf_op jit(solution)/shard_map/ppermute | solution.py:10
  181.0 30.1 %all-gather.1 = f32[8,1,8]{2,1,0:T(1,128)S(1)} all-gather(f32[1,1,8]{2,1,0:T(1,128)S(1)} %bitcast.199), channel_id=1, replica_groups=mesh['az'=32,'rad'=8] {'rad'}, dimensions={0}, use_global_device_ids=true | all-gather | bytes 288 | tf_op jit(solution)/shard_map/all_gather | solution.py:107
  211.3 23.7 %all-gather.2 = f32[8,4,8]{2,1,0:T(4,128)S(1)} all-gather(f32[1,4,8]{2,1,0:T(4,128)S(1)} %maximum_bitcast_fusion.1), channel_id=2, replica_groups=mesh['az'=32,'rad'=8] {'rad'}, dimensions={0}, use_global_device_ids=true | all-gather | bytes 1152 | tf_op jit(solution)/shard_map/all_gather | solution.py:106
  235.0 0.6 multiply_bitcast_fusion.2
  239.6 32.1 %collective-permute-done.5 = f32[5,8,64,128]{3,2,1,0:T(8,128)S(1)} collective-permute-done((f32[5,8,64,128]{3,2,1,0:T(8,128)S(1)}, f32[5,8,64,128]{3,2,1,0:T(8,128)S(1)}, u32[]{:S(2)}, u32[]{:S(2)}) %collective-permute-start.5) | collective-permute-done | bytes 1310752 | tf_op jit(solution)/shard_map/ppermute | solution.py:10
  271.9 48.9 %copy.70 = f32[5,8,64,256]{1,0,2,3:T(8,128)} copy(f32[5,8,64,256]{3,2,1,0:T(8,128)S(1)} %pad_maximum_fusion.4) | data formatting | bytes 5242880 | tf_op jit(solution)/shard_map/concatenate | solution.py:77
  320.8 24.3 %gather_fusion = f32[64,5,8,128]{2,1,3,0:T(8,128)} fusion(f32[64,5,8,256]{2,1,0,3:T(8,128)} %bitcast, s32[64]{0:T(128)S(1)} %get-tuple-element.40), kind=kCustom, calls=%fused_computation | custom fusion | bytes 2622464 | tf_op jit(solution)/shard_map/vmap()/gather | solution.py:79
  345.1 13.7 %copy.71 = f32[64,5,8,128]{3,0,2,1:T(8,128)S(1)} copy(f32[64,5,8,128]{2,1,3,0:T(8,128)} %gather_fusion) | data formatting | bytes 2621440 | tf_op jit(solution)/shard_map/vmap()/gather | solution.py:79
  358.9 1.8 slice_maximum_fusion
  360.6 1.9 copy.72
  363.9 6.0 %collective-permute-start.7 = (f32[6,8,64,1]{2,1,3,0:T(8,128)S(1)}, f32[6,8,64,1]{2,1,3,0:T(8,128)S(1)}, u32[]{:S(2)}, u32[]{:S(2)}) collective-permute-start(f32[6,8,64,1]{2,1,3,0:T(8,128)S(1)} %copy.74), channel_id=1, source_target_pairs={{8,0},{16,8},{24,16},{32,24},{40,32},{48,40},{56,48},{64,56},{72,6... | collective-permute-start | bytes 36872 | tf_op jit(solution)/shard_map/ppermute | solution.py:21
  370.8 1.0 maximum_bitcast_fusion
  371.8 0.8 minimum_bitcast_fusion
  372.7 1.7 copy.75
  374.4 2.3 fusion.1
  378.0 28.1 %all_gather.13 = f32[8,8,128]{2,0,1:T(8,128)S(1)} all-gather(f32[8,1,128]{2,0,1:T(8,128)S(1)} %bitcast.178), channel_id=1, replica_groups=mesh['az'=32,'rad'=8] {'rad'}, dimensions={1}, use_global_device_ids=true | all-gather | bytes 36864 | tf_op jit(solution)/shard_map/all_gather | solution.py:105
  406.1 28.0 %all_gather.15 = f32[8,8,128]{2,0,1:T(8,128)S(1)} all-gather(f32[8,1,128]{2,0,1:T(8,128)S(1)} %bitcast.177), channel_id=1, replica_groups=mesh['az'=32,'rad'=8] {'rad'}, dimensions={1}, use_global_device_ids=true | all-gather | bytes 36864 | tf_op jit(solution)/shard_map/all_gather | solution.py:104
  435.4 1.1 pad_maximum_fusion.6
  (136 shorter events, 10.7 us)
Async XLA Ops:
  0.0 26.2 %collective-permute-start = (f32[5,8,64,128]{3,2,1,0:T(8,128)}, f32[5,8,64,128]{3,2,1,0:T(8,128)S(1)}, u32[]{:S(2)}, u32[]{:S(2)}) collective-permute-start(f32[5,8,64,128]{3,2,1,0:T(8,128)} %param.5), channel_id=1, source_target_pairs={{248,0},{0,8},{8,16},{16,24},{24,32},{32,40},{40,48},{48,56},{56,6... | collective-permute-start | bytes 3932168 | tf_op jit(solution)/shard_map/ppermute | solution.py:10
  27.8 38.1 %collective-permute-start.1 = (f32[5,8,64,128]{3,2,1,0:T(8,128)S(1)}, f32[5,8,64,128]{3,2,1,0:T(8,128)S(1)}, u32[]{:S(2)}, u32[]{:S(2)}) collective-permute-start(f32[5,8,64,128]{3,2,1,0:T(8,128)S(1)} %broadcast_select_fusion), channel_id=1, source_target_pairs={{240,0},{248,8},{0,16},{8,24},{16,32},{24,40},{32,48},{40,56},{48,... | collective-permute-start | bytes 3932168 | tf_op jit(solution)/shard_map/ppermute | solution.py:10
  66.3 73.0 %collective-permute-start.2 = (f32[5,8,64,128]{3,2,1,0:T(8,128)S(1)}, f32[5,8,64,128]{3,2,1,0:T(8,128)S(1)}, u32[]{:S(2)}, u32[]{:S(2)}) collective-permute-start(f32[5,8,64,128]{3,2,1,0:T(8,128)S(1)} %broadcast_select_fusion.1), channel_id=1, source_target_pairs={{224,0},{232,8},{240,16},{248,24},{0,32},{8,40},{16,48},{24,56},{3... | collective-permute-start | bytes 3932168 | tf_op jit(solution)/shard_map/ppermute | solution.py:10
  139.6 40.1 %collective-permute-start.3 = (f32[5,8,64,128]{3,2,1,0:T(8,128)S(1)}, f32[5,8,64,128]{3,2,1,0:T(8,128)S(1)}, u32[]{:S(2)}, u32[]{:S(2)}) collective-permute-start(f32[5,8,64,128]{3,2,1,0:T(8,128)S(1)} %broadcast_select_fusion.2), channel_id=1, source_target_pairs={{192,0},{200,8},{208,16},{216,24},{224,32},{232,40},{240,48},{248,... | collective-permute-start | bytes 3932168 | tf_op jit(solution)/shard_map/ppermute | solution.py:10
  179.9 56.8 %collective-permute-start.4 = (f32[5,8,64,128]{3,2,1,0:T(8,128)S(1)}, f32[5,8,64,128]{3,2,1,0:T(8,128)S(1)}, u32[]{:S(2)}, u32[]{:S(2)}) collective-permute-start(f32[5,8,64,128]{3,2,1,0:T(8,128)S(1)} %broadcast_select_fusion.3), channel_id=1, source_target_pairs={{128,0},{136,8},{144,16},{152,24},{160,32},{168,40},{176,48},{184,... | collective-permute-start | bytes 3932168 | tf_op jit(solution)/shard_map/ppermute | solution.py:10
  237.0 34.7 %collective-permute-start.5 = (f32[5,8,64,128]{3,2,1,0:T(8,128)S(1)}, f32[5,8,64,128]{3,2,1,0:T(8,128)S(1)}, u32[]{:S(2)}, u32[]{:S(2)}) collective-permute-start(f32[5,8,64,128]{3,2,1,0:T(8,128)S(1)} %broadcast_select_fusion.4), channel_id=1, source_target_pairs={{248,0},{0,8},{8,16},{16,24},{24,32},{32,40},{40,48},{48,56},{56,6... | collective-permute-start | bytes 3932168 | tf_op jit(solution)/shard_map/ppermute | solution.py:10
  362.6 7.7 %collective-permute-start.6 = (f32[6,8,64,1]{2,1,3,0:T(8,128)S(1)}, f32[6,8,64,1]{2,1,3,0:T(8,128)S(1)}, u32[]{:S(2)}, u32[]{:S(2)}) collective-permute-start(f32[6,8,64,1]{2,1,3,0:T(8,128)S(1)} %copy.72), channel_id=1, source_target_pairs={{0,8},{8,16},{16,24},{24,32},{32,40},{40,48},{48,56},{56,64},{64,7... | collective-permute-start | bytes 36872 | tf_op jit(solution)/shard_map/ppermute | solution.py:20
  363.9 8.7 %collective-permute-start.7 = (f32[6,8,64,1]{2,1,3,0:T(8,128)S(1)}, f32[6,8,64,1]{2,1,3,0:T(8,128)S(1)}, u32[]{:S(2)}, u32[]{:S(2)}) collective-permute-start(f32[6,8,64,1]{2,1,3,0:T(8,128)S(1)} %copy.74), channel_id=1, source_target_pairs={{8,0},{16,8},{24,16},{32,24},{40,32},{48,40},{56,48},{64,56},{72,6... | collective-permute-start | bytes 36872 | tf_op jit(solution)/shard_map/ppermute | solution.py:21
  377.6 56.6 %copy-start.3 = (f32[8,1]{0,1:T(1,128)S(1)}, f32[8,1]{0,1:T(1,128)}, u32[]{:S(2)}) copy-start(f32[8,1]{0,1:T(1,128)} %copy-done.2) | copy-start | bytes 100
  377.6 56.5 %copy-start.5 = (f32[8,1]{0,1:T(1,128)S(1)}, f32[8,1]{0,1:T(1,128)}, u32[]{:S(2)}) copy-start(f32[8,1]{0,1:T(1,128)} %copy-done.4) | copy-start | bytes 100
  377.6 56.5 %copy-start.7 = (f32[8,1]{0,1:T(1,128)S(1)}, f32[8,1]{0,1:T(1,128)}, u32[]{:S(2)}) copy-start(f32[8,1]{0,1:T(1,128)} %copy-done.6) | copy-start | bytes 100
  377.6 56.5 %copy-start.8 = (f32[8]{0:T(128)S(1)}, f32[8]{0:T(128)}, u32[]{:S(2)}) copy-start(f32[8]{0:T(128)} %get-tuple-element.53) | copy-start | bytes 100
  377.6 56.5 %copy-start.9 = (f32[8]{0:T(128)S(1)}, f32[8]{0:T(128)}, u32[]{:S(2)}) copy-start(f32[8]{0:T(128)} %get-tuple-element.63) | copy-start | bytes 100
  377.7 56.5 %copy-start.10 = (f32[8]{0:T(128)S(1)}, f32[8]{0:T(128)}, u32[]{:S(2)}) copy-start(f32[8]{0:T(128)} %get-tuple-element.55) | copy-start | bytes 100
  377.7 56.5 %copy-start.11 = (f32[8]{0:T(128)S(1)}, f32[8]{0:T(128)}, u32[]{:S(2)}) copy-start(f32[8]{0:T(128)} %get-tuple-element.64) | copy-start | bytes 100
  377.7 56.5 %copy-start.12 = (f32[8]{0:T(128)S(1)}, f32[8]{0:T(128)}, u32[]{:S(2)}) copy-start(f32[8]{0:T(128)} %get-tuple-element.57) | copy-start | bytes 100
  377.8 56.7 %copy-start.19 = (f32[8,1]{0,1:T(1,128)S(1)}, f32[8,1]{0,1:T(1,128)}, u32[]{:S(2)}) copy-start(f32[8,1]{0,1:T(1,128)} %copy-done.18) | copy-start | bytes 100
  377.9 56.8 %copy-start.42 = (f32[8]{0:T(128)S(1)}, f32[8]{0:T(128)}, u32[]{:S(2)}) copy-start(f32[8]{0:T(128)} %multiply_bitcast_fusion.8) | copy-start | bytes 100
  377.9 56.9 %copy-start.40 = (f32[8]{0:T(128)S(1)}, f32[8]{0:T(128)}, u32[]{:S(2)}) copy-start(f32[8]{0:T(128)} %get-tuple-element.92) | copy-start | bytes 100
  377.9 56.9 %copy-start.39 = (f32[8]{0:T(128)S(1)}, f32[8]{0:T(128)}, u32[]{:S(2)}) copy-start(f32[8]{0:T(128)} %get-tuple-element.91) | copy-start | bytes 100
  377.9 57.0 %copy-start.37 = (f32[8]{0:T(128)S(1)}, f32[8]{0:T(128)}, u32[]{:S(2)}) copy-start(f32[8]{0:T(128)} %get-tuple-element.82) | copy-start | bytes 100
  377.9 57.1 %copy-start.36 = (f32[8]{0:T(128)S(1)}, f32[8]{0:T(128)}, u32[]{:S(2)}) copy-start(f32[8]{0:T(128)} %get-tuple-element.90) | copy-start | bytes 100
  377.9 57.1 %copy-start.21 = (f32[8,1]{0,1:T(1,128)S(1)}, f32[8,1]{0,1:T(1,128)}, u32[]{:S(2)}) copy-start(f32[8,1]{0,1:T(1,128)} %copy-done.20) | copy-start | bytes 100
  377.9 57.1 %copy-start.41 = (f32[8]{0:T(128)S(1)}, f32[8]{0:T(128)}, u32[]{:S(2)}) copy-start(f32[8]{0:T(128)} %get-tuple-element.9) | copy-start | bytes 100
  (27 other events, 938.6 us)
where the time goes:
time: 437 us
  waiting for transfers between devices  168 us (38%)
  blocking collectives  110 us (25%)
  local copies, waits for them, and re-layouts  93.7 us (21%)
  starting transfers between devices  47.4 us (11%)
  other arithmetic  16.2 us (4%)
    ppermute x6, waiting for transfers between devices, shifted(): return lax.ppermute(block, axis, route)  168 us
    concatenate x1, local copies, waits for them, and re-layouts, per_device(): joined = jnp.concatenate([previous, moving], axis=3)  48.9 us
    ppermute x6, starting transfers between devices, shifted(): return lax.ppermute(block, axis, route)  41.2 us
    gather x2, local copies, waits for them, and re-layouts, per_device(): lax.dynamic_slice_in_dim(one_row, opening, shard_cells, axis=-1)  38 us
    all_gather x1, blocking collectives, per_device(): lax.all_gather(coupling, 'rad', axis=1, tiled=True)  30.1 us
    all_gather x1, blocking collectives, per_device(): lax.all_gather(local_part[:, -1:, :], 'rad', axis=1, tiled=True)  28.1 us
    all_gather x1, blocking collectives, per_device(): lax.all_gather(local_part[:, :1, :], 'rad', axis=1, tiled=True)  28 us
    all_gather x1, blocking collectives, per_device(): lax.all_gather(corners, 'rad', axis=1, tiled=True)  23.7 us
  transfers between devices with their start and end apart: 8, of which 6 were waited for; matrix products, arithmetic and copies ran while one was open for 2% of the time, Pallas kernels for 0%

commit v1 on v0

--- a/solution.py
+++ b/solution.py
@@ -103,7 +103,9 @@
     first_all, last_all, corner_all, link_all = (
         lax.all_gather(local_part[:, :1, :], "rad", axis=1, tiled=True),
         lax.all_gather(local_part[:, -1:, :], "rad", axis=1, tiled=True),
-        lax.all_gather(corners, "rad", axis=1, tiled=True),
+        jnp.concatenate(
+            lax.all_to_all(jnp.stack([corners] * lax.axis_size("rad")), "rad", 0, 0), axis=1
+        ),
         lax.all_gather(coupling, "rad", axis=1, tiled=True),
     )
     before, beyond = interface_solve(

time: 437 us -> 420 us (0.961)
  blocking collectives: 110 us -> 75.4 us
  starting transfers between devices: 47.4 us -> 74.3 us
  waiting for transfers between devices: 168 us -> 151 us
  local copies, waits for them, and re-layouts: 93.7 us -> 99.6 us
    all_to_all x0 -> x1, starting transfers between devices: none -> 26.8 us  [per_device(): lax.all_to_all(jnp.stack([corners] * lax.axis_size('rad')), 'rad', 0, 0)]
    all_gather x1 -> x0, blocking collectives: 23.7 us -> none  [per_device(): lax.all_gather(corners, 'rad', axis=1, tiled=True)]
    ppermute x6, waiting for transfers between devices: 168 us -> 150 us  [shifted(): return lax.ppermute(block, axis, route)]
    all_gather x1, blocking collectives: 30.1 us -> 19.1 us  [per_device(): lax.all_gather(coupling, 'rad', axis=1, tiled=True)]
    unnamed x90 -> x118, local copies, waits for them, and re-layouts: 1.63 us -> 6.09 us
  transfers between devices with their start and end apart: 8 -> 9, of which waited for: 6 -> 6; matrix products, arithmetic and copies ran while one was open for 2% -> 4% of each run, Pallas kernels for 0% -> 0%
where the time goes in v1:
time: 420 us
  waiting for transfers between devices  151 us (36%)
  local copies, waits for them, and re-layouts  99.6 us (24%)
  blocking collectives  75.4 us (18%)
  starting transfers between devices  74.3 us (18%)
  other arithmetic  19 us (5%)
    ppermute x6, waiting for transfers between devices, shifted(): return lax.ppermute(block, axis, route)  150 us
    concatenate x1, local copies, waits for them, and re-layouts, per_device(): joined = jnp.concatenate([previous, moving], axis=3)  48.9 us
    ppermute x6, starting transfers between devices, shifted(): return lax.ppermute(block, axis, route)  41.2 us
    gather x2, local copies, waits for them, and re-layouts, per_device(): lax.dynamic_slice_in_dim(one_row, opening, shard_cells, axis=-1)  38 us
    all_gather x1, blocking collectives, per_device(): lax.all_gather(local_part[:, -1:, :], 'rad', axis=1, tiled=True)  28.2 us
    all_gather x1, blocking collectives, per_device(): lax.all_gather(local_part[:, :1, :], 'rad', axis=1, tiled=True)  28 us
    all_to_all x1, starting transfers between devices, per_device(): lax.all_to_all(jnp.stack([corners] * lax.axis_size('rad')), 'rad', 0, 0)  26.8 us
    all_gather x1, blocking collectives, per_device(): lax.all_gather(coupling, 'rad', axis=1, tiled=True)  19.1 us
  transfers between devices with their start and end apart: 9, of which 6 were waited for; matrix products, arithmetic and copies ran while one was open for 4% of the time, Pallas kernels for 0%

profile of v1, /device:TPU:0, one launch (start us, length us, event | category | flops | bytes accessed | tf_op | source)
XLA Modules:
  0.0 419.8 jit_solution(15379997158447839926)
XLA Ops:
  0.7 25.5 %collective-permute-done = f32[5,8,64,128]{3,2,1,0:T(8,128)S(1)} collective-permute-done((f32[5,8,64,128]{3,2,1,0:T(8,128)}, f32[5,8,64,128]{3,2,1,0:T(8,128)S(1)}, u32[]{:S(2)}, u32[]{:S(2)}) %collective-permute-start) | collective-permute-done | bytes 1310752 | tf_op jit(solution)/shard_map/ppermute | solution.py:10
  26.2 1.6 broadcast_select_fusion
  27.9 38.1 %collective-permute-done.1 = f32[5,8,64,128]{3,2,1,0:T(8,128)S(1)} collective-permute-done((f32[5,8,64,128]{3,2,1,0:T(8,128)S(1)}, f32[5,8,64,128]{3,2,1,0:T(8,128)S(1)}, u32[]{:S(2)}, u32[]{:S(2)}) %collective-permute-start.1) | collective-permute-done | bytes 1310752 | tf_op jit(solution)/shard_map/ppermute | solution.py:10
  66.3 40.9 %collective-permute-start.2 = (f32[5,8,64,128]{3,2,1,0:T(8,128)S(1)}, f32[5,8,64,128]{3,2,1,0:T(8,128)S(1)}, u32[]{:S(2)}, u32[]{:S(2)}) collective-permute-start(f32[5,8,64,128]{3,2,1,0:T(8,128)S(1)} %broadcast_select_fusion.1), channel_id=1, source_target_pairs={{224,0},{232,8},{240,16},{248,24},{0,32},{8,40},{16,48},{24,56},{3... | collective-permute-start | bytes 3932168 | tf_op jit(solution)/shard_map/ppermute | solution.py:10
  107.1 32.1 %collective-permute-done.2 = f32[5,8,64,128]{3,2,1,0:T(8,128)S(1)} collective-permute-done((f32[5,8,64,128]{3,2,1,0:T(8,128)S(1)}, f32[5,8,64,128]{3,2,1,0:T(8,128)S(1)}, u32[]{:S(2)}, u32[]{:S(2)}) %collective-permute-start.2) | collective-permute-done | bytes 1310752 | tf_op jit(solution)/shard_map/ppermute | solution.py:10
  141.1 26.8 %all-to-all-start = ((f32[8,8,1,4]{1,3,2,0:T(4,128)}), f32[8,8,1,4]{1,3,2,0:T(4,128)S(1)}, u32[]{:S(2)}, u32[]{:S(2)}) async-start(f32[8,8,1,4]{1,3,2,0:T(4,128)} %stack.9), calls=%async_computation | async-start | bytes 32768 | tf_op jit(solution)/shard_map/all_to_all | solution.py:107
  168.6 1.1 copy.103
  169.9 19.1 %all-gather = f32[8,1,8]{2,1,0:T(1,128)S(1)} all-gather(f32[1,1,8]{2,1,0:T(1,128)S(1)} %bitcast.160), channel_id=1, replica_groups=mesh['az'=32,'rad'=8] {'rad'}, dimensions={0}, use_global_device_ids=true | all-gather | bytes 288 | tf_op jit(solution)/shard_map/all_gather | solution.py:109
  189.8 1.1 copy-done.3
  190.9 1.6 broadcast_select_fusion.3
  196.6 22.2 %collective-permute-done.4 = f32[5,8,64,128]{3,2,1,0:T(8,128)S(1)} collective-permute-done((f32[5,8,64,128]{3,2,1,0:T(8,128)S(1)}, f32[5,8,64,128]{3,2,1,0:T(8,128)S(1)}, u32[]{:S(2)}, u32[]{:S(2)}) %collective-permute-start.4) | collective-permute-done | bytes 1310752 | tf_op jit(solution)/shard_map/ppermute | solution.py:10
  222.4 32.2 %collective-permute-done.5 = f32[5,8,64,128]{3,2,1,0:T(8,128)S(1)} collective-permute-done((f32[5,8,64,128]{3,2,1,0:T(8,128)S(1)}, f32[5,8,64,128]{3,2,1,0:T(8,128)S(1)}, u32[]{:S(2)}, u32[]{:S(2)}) %collective-permute-start.5) | collective-permute-done | bytes 1310752 | tf_op jit(solution)/shard_map/ppermute | solution.py:10
  254.8 48.9 %copy.66 = f32[5,8,64,256]{1,0,2,3:T(8,128)} copy(f32[5,8,64,256]{3,2,1,0:T(8,128)S(1)} %pad_maximum_fusion.4) | data formatting | bytes 5242880 | tf_op jit(solution)/shard_map/concatenate | solution.py:77
  303.7 24.3 %gather_fusion = f32[64,5,8,128]{2,1,3,0:T(8,128)} fusion(f32[64,5,8,256]{2,1,0,3:T(8,128)} %bitcast, s32[64]{0:T(128)S(1)} %get-tuple-element.47), kind=kCustom, calls=%fused_computation | custom fusion | bytes 2622464 | tf_op jit(solution)/shard_map/vmap()/gather | solution.py:79
  328.0 13.7 %copy.67 = f32[64,5,8,128]{3,0,2,1:T(8,128)S(1)} copy(f32[64,5,8,128]{2,1,3,0:T(8,128)} %gather_fusion) | data formatting | bytes 2621440 | tf_op jit(solution)/shard_map/vmap()/gather | solution.py:79
  341.7 1.8 slice_maximum_fusion
  343.5 1.9 copy.68
  346.7 6.0 %collective-permute-start.7 = (f32[6,8,64,1]{2,1,3,0:T(8,128)S(1)}, f32[6,8,64,1]{2,1,3,0:T(8,128)S(1)}, u32[]{:S(2)}, u32[]{:S(2)}) collective-permute-start(f32[6,8,64,1]{2,1,3,0:T(8,128)S(1)} %copy.70), channel_id=1, source_target_pairs={{8,0},{16,8},{24,16},{32,24},{40,32},{48,40},{56,48},{64,56},{72,6... | collective-permute-start | bytes 36872 | tf_op jit(solution)/shard_map/ppermute | solution.py:21
  353.7 1.0 maximum_bitcast_fusion
  355.6 1.7 copy.71
  357.3 2.3 fusion.1
  361.2 28.2 %all_gather.10 = f32[8,8,128]{2,0,1:T(8,128)S(1)} all-gather(f32[8,1,128]{2,0,1:T(8,128)S(1)} %bitcast.129), channel_id=1, replica_groups=mesh['az'=32,'rad'=8] {'rad'}, dimensions={1}, use_global_device_ids=true | all-gather | bytes 36864 | tf_op jit(solution)/shard_map/all_gather | solution.py:105
  389.4 28.0 %all_gather.11 = f32[8,8,128]{2,0,1:T(8,128)S(1)} all-gather(f32[8,1,128]{2,0,1:T(8,128)S(1)} %bitcast.128), channel_id=1, replica_groups=mesh['az'=32,'rad'=8] {'rad'}, dimensions={1}, use_global_device_ids=true | all-gather | bytes 36864 | tf_op jit(solution)/shard_map/all_gather | solution.py:104
  418.7 1.1 pad_maximum_fusion.6
  (173 shorter events, 17.8 us)
Async XLA Ops:
  0.0 26.2 %collective-permute-start = (f32[5,8,64,128]{3,2,1,0:T(8,128)}, f32[5,8,64,128]{3,2,1,0:T(8,128)S(1)}, u32[]{:S(2)}, u32[]{:S(2)}) collective-permute-start(f32[5,8,64,128]{3,2,1,0:T(8,128)} %param.5), channel_id=1, source_target_pairs={{248,0},{0,8},{8,16},{16,24},{24,32},{32,40},{40,48},{48,56},{56,6... | collective-permute-start | bytes 3932168 | tf_op jit(solution)/shard_map/ppermute | solution.py:10
  27.8 38.1 %collective-permute-start.1 = (f32[5,8,64,128]{3,2,1,0:T(8,128)S(1)}, f32[5,8,64,128]{3,2,1,0:T(8,128)S(1)}, u32[]{:S(2)}, u32[]{:S(2)}) collective-permute-start(f32[5,8,64,128]{3,2,1,0:T(8,128)S(1)} %broadcast_select_fusion), channel_id=1, source_target_pairs={{240,0},{248,8},{0,16},{8,24},{16,32},{24,40},{32,48},{40,56},{48,... | collective-permute-start | bytes 3932168 | tf_op jit(solution)/shard_map/ppermute | solution.py:10
  66.3 73.0 %collective-permute-start.2 = (f32[5,8,64,128]{3,2,1,0:T(8,128)S(1)}, f32[5,8,64,128]{3,2,1,0:T(8,128)S(1)}, u32[]{:S(2)}, u32[]{:S(2)}) collective-permute-start(f32[5,8,64,128]{3,2,1,0:T(8,128)S(1)} %broadcast_select_fusion.1), channel_id=1, source_target_pairs={{224,0},{232,8},{240,16},{248,24},{0,32},{8,40},{16,48},{24,56},{3... | collective-permute-start | bytes 3932168 | tf_op jit(solution)/shard_map/ppermute | solution.py:10
  139.5 50.3 %collective-permute-start.3 = (f32[5,8,64,128]{3,2,1,0:T(8,128)S(1)}, f32[5,8,64,128]{3,2,1,0:T(8,128)S(1)}, u32[]{:S(2)}, u32[]{:S(2)}) collective-permute-start(f32[5,8,64,128]{3,2,1,0:T(8,128)S(1)} %broadcast_select_fusion.2), channel_id=1, source_target_pairs={{192,0},{200,8},{208,16},{216,24},{224,32},{232,40},{240,48},{248,... | collective-permute-start | bytes 3932168 | tf_op jit(solution)/shard_map/ppermute | solution.py:10
  141.1 48.7 %all-to-all-start = ((f32[8,8,1,4]{1,3,2,0:T(4,128)}), f32[8,8,1,4]{1,3,2,0:T(4,128)S(1)}, u32[]{:S(2)}, u32[]{:S(2)}) async-start(f32[8,8,1,4]{1,3,2,0:T(4,128)} %stack.9), calls=%async_computation | async-start | bytes 32768 | tf_op jit(solution)/shard_map/all_to_all | solution.py:107
  192.4 26.4 %collective-permute-start.4 = (f32[5,8,64,128]{3,2,1,0:T(8,128)S(1)}, f32[5,8,64,128]{3,2,1,0:T(8,128)S(1)}, u32[]{:S(2)}, u32[]{:S(2)}) collective-permute-start(f32[5,8,64,128]{3,2,1,0:T(8,128)S(1)} %broadcast_select_fusion.3), channel_id=1, source_target_pairs={{128,0},{136,8},{144,16},{152,24},{160,32},{168,40},{176,48},{184,... | collective-permute-start | bytes 3932168 | tf_op jit(solution)/shard_map/ppermute | solution.py:10
  219.1 35.5 %collective-permute-start.5 = (f32[5,8,64,128]{3,2,1,0:T(8,128)S(1)}, f32[5,8,64,128]{3,2,1,0:T(8,128)S(1)}, u32[]{:S(2)}, u32[]{:S(2)}) collective-permute-start(f32[5,8,64,128]{3,2,1,0:T(8,128)S(1)} %broadcast_select_fusion.4), channel_id=1, source_target_pairs={{248,0},{0,8},{8,16},{16,24},{24,32},{32,40},{40,48},{48,56},{56,6... | collective-permute-start | bytes 3932168 | tf_op jit(solution)/shard_map/ppermute | solution.py:10
  345.5 7.7 %collective-permute-start.6 = (f32[6,8,64,1]{2,1,3,0:T(8,128)S(1)}, f32[6,8,64,1]{2,1,3,0:T(8,128)S(1)}, u32[]{:S(2)}, u32[]{:S(2)}) collective-permute-start(f32[6,8,64,1]{2,1,3,0:T(8,128)S(1)} %copy.68), channel_id=1, source_target_pairs={{0,8},{8,16},{16,24},{24,32},{32,40},{40,48},{48,56},{56,64},{64,7... | collective-permute-start | bytes 36872 | tf_op jit(solution)/shard_map/ppermute | solution.py:20
  346.7 8.9 %collective-permute-start.7 = (f32[6,8,64,1]{2,1,3,0:T(8,128)S(1)}, f32[6,8,64,1]{2,1,3,0:T(8,128)S(1)}, u32[]{:S(2)}, u32[]{:S(2)}) collective-permute-start(f32[6,8,64,1]{2,1,3,0:T(8,128)S(1)} %copy.70), channel_id=1, source_target_pairs={{8,0},{16,8},{24,16},{32,24},{40,32},{48,40},{56,48},{64,56},{72,6... | collective-permute-start | bytes 36872 | tf_op jit(solution)/shard_map/ppermute | solution.py:21
  360.5 56.9 %copy-start.4 = (f32[8]{0:T(128)S(1)}, f32[8]{0:T(128)}, u32[]{:S(2)}) copy-start(f32[8]{0:T(128)} %get-tuple-element.70) | copy-start | bytes 100
  360.5 56.9 %copy-start.5 = (f32[8]{0:T(128)S(1)}, f32[8]{0:T(128)}, u32[]{:S(2)}) copy-start(f32[8]{0:T(128)} %get-tuple-element.76) | copy-start | bytes 100
  360.5 56.9 %copy-start.6 = (f32[8]{0:T(128)S(1)}, f32[8]{0:T(128)}, u32[]{:S(2)}) copy-start(f32[8]{0:T(128)} %get-tuple-element.77) | copy-start | bytes 100
  360.6 56.9 %copy-start.7 = (f32[8]{0:T(128)S(1)}, f32[8]{0:T(128)}, u32[]{:S(2)}) copy-start(f32[8]{0:T(128)} %get-tuple-element.74) | copy-start | bytes 100
  360.6 56.9 %copy-start.8 = (f32[8]{0:T(128)S(1)}, f32[8]{0:T(128)}, u32[]{:S(2)}) copy-start(f32[8]{0:T(128)} %get-tuple-element.81) | copy-start | bytes 100
  360.6 56.9 %copy-start.9 = (f32[8,1]{0,1:T(1,128)S(1)}, f32[8,1]{0,1:T(1,128)}, u32[]{:S(2)}) copy-start(f32[8,1]{0,1:T(1,128)} %get-tuple-element.11) | copy-start | bytes 100
  360.8 57.1 %copy-start.24 = (f32[8,1]{0,1:T(1,128)S(1)}, f32[8,1]{0,1:T(1,128)}, u32[]{:S(2)}) copy-start(f32[8,1]{0,1:T(1,128)} %copy-done.23) | copy-start | bytes 100
  360.8 57.2 %copy-start.42 = (f32[8]{0:T(128)S(1)}, f32[8]{0:T(128)}, u32[]{:S(2)}) copy-start(f32[8]{0:T(128)} %multiply_bitcast_fusion.15) | copy-start | bytes 100
  360.8 57.3 %copy-start.43 = (f32[8]{0:T(128)S(1)}, f32[8]{0:T(128)}, u32[]{:S(2)}) copy-start(f32[8]{0:T(128)} %multiply_bitcast_fusion.12) | copy-start | bytes 100
  360.8 57.3 %copy-start.41 = (f32[8]{0:T(128)S(1)}, f32[8]{0:T(128)}, u32[]{:S(2)}) copy-start(f32[8]{0:T(128)} %multiply_bitcast_fusion.9) | copy-start | bytes 100
  360.8 57.4 %copy-start.40 = (f32[8]{0:T(128)S(1)}, f32[8]{0:T(128)}, u32[]{:S(2)}) copy-start(f32[8]{0:T(128)} %multiply_bitcast_fusion.6) | copy-start | bytes 100
  360.8 57.5 %copy-start.39 = (f32[8]{0:T(128)S(1)}, f32[8]{0:T(128)}, u32[]{:S(2)}) copy-start(f32[8]{0:T(128)} %multiply_bitcast_fusion.4) | copy-start | bytes 100
  360.8 57.5 %copy-start.34 = (f32[8]{0:T(128)S(1)}, f32[8]{0:T(128)}, u32[]{:S(2)}) copy-start(f32[8]{0:T(128)} %get-tuple-element.9) | copy-start | bytes 100
  360.8 57.5 %copy-start.35 = (f32[8,1]{0,1:T(1,128)S(1)}, f32[8,1]{0,1:T(1,128)}, u32[]{:S(2)}) copy-start(f32[8,1]{0,1:T(1,128)} %get-tuple-element.12) | copy-start | bytes 100
  361.2 57.5 %slice-start = ((f32[5,8,64,128]{3,2,1,0:T(8,128)}), f32[4,8,64,128]{3,2,1,0:T(8,128)S(1)}, s32[]{:S(2)}) async-start(f32[5,8,64,128]{3,2,1,0:T(8,128)} %copy-done), calls=%async_computation.1 | async-start | bytes 2097152 | tf_op jit(solution)/shard_map/slice | solution.py:131
  (30 other events, 1240.5 us)
